TPU v7x, 256 devices: a whole 4x4x8 slice. The times are simulated.
256 devices in a mesh: group: 8 (over x, core), expert: 32 (over z, y).
Axes of the slice: x: 4, y: 4, z: 8, core: 2. Of those that a mesh axis runs over, the one named last changes fastest.
Arguments:
- out_grad: bfloat16 [65536, 3584], P(('group', 'expert')), may hold values from -6 to 6
- gates: float32 [65536, 8], P(('group', 'expert')), may hold values from 0.05 to 0.6
- routes: int32 [65536, 8], P(('group', 'expert')), may hold values from 0 to 95, all different within a row
- copy_pick: int32 [65536, 8], P(('group', 'expert')), may hold values from 0 to 839
- replica_plan: int32 [32], replicated, may hold values from 0 to 23, as said below
- down_weight: bfloat16 [32, 1024, 3584], P('expert'), as said below
- saved_hidden: bfloat16 [8, 32, 32, 20, 1024], P('group', 'expert'), may hold values from -0.75 to 0.75
Outputs:
- route_grad: float32 [65536, 8], P(('group', 'expert'))
- hidden_grad: bfloat16 [8, 32, 32, 20, 1024], P('group', 'expert')
- copy_grad: bfloat16 [32, 1024, 3584], P('expert', 'group')
Inputs may be any that keep to these rules, and one draw needn't show every extreme that they name: `replica_plan`: every expert 0 to 23 is served by at least one slot; exactly 2 experts are served by more than one slot. `down_weight`: slots that serve the same expert hold equal weights.
All inputs are finite; a program needn't handle non-finite values.
Results may differ from a plain program's by a relative error of at most 0.019.
Values may be sent and summed in bfloat16 or wider, within the bound.
A program may use at most 128 MiB of HBM per device.

v0:
```python
import jax
import jax.numpy as jnp
from jax import lax
from jax.sharding import PartitionSpec as P

HOT = 2


def slot_layout(replica_plan):
    slot_count = replica_plan.shape[0]
    slot_ids = jnp.arange(slot_count, dtype=jnp.int32)
    same_expert = replica_plan[:, None] == replica_plan[None, :]
    earlier_slot = slot_ids[None, :] < slot_ids[:, None]
    ordinal = jnp.sum(same_expert & earlier_slot, axis=1)
    return (slot_ids, same_expert, ordinal)


def route_slots(routes, copy_pick, replica_plan, expert_count):
    slot_ids, same_expert, ordinal = slot_layout(replica_plan)
    serves = replica_plan == routes[..., None]
    copies = jnp.sum(serves, axis=-1)
    inside = routes < expert_count
    chosen = copy_pick % jnp.maximum(copies, 1)
    slot_match = serves & (ordinal == chosen[..., None]) & inside[..., None]
    slot_of = jnp.sum(jnp.where(slot_match, slot_ids, 0), axis=-1)
    return (slot_match, slot_of, inside)


def route_ranks(slot_match):
    onehot = slot_match.astype(jnp.int32)
    earlier = jnp.cumsum(onehot, axis=-2) - onehot
    return jnp.sum(earlier * onehot, axis=-1)


def local(out_grad, gates, routes, copy_pick, replica_plan, down_weight, saved_hidden):
    slot_count = replica_plan.shape[0]
    cap_rows = saved_hidden.shape[3]
    expert_count = slot_count - slot_count // 4
    tok_dev, top_count = routes.shape
    model_width = out_grad.shape[1]
    hidden_units = down_weight.shape[1]
    route_count = tok_dev * top_count
    held_count = slot_count * cap_rows
    slot_match, slot_of, inside = route_slots(routes, copy_pick, replica_plan, expert_count)
    route_rank = route_ranks(slot_match.reshape(route_count, slot_count))
    kept_route = inside.reshape(-1) & (route_rank < cap_rows)
    position = jnp.where(kept_route, slot_of.reshape(-1) * cap_rows + route_rank, held_count)
    source_route = (
        jnp.full((held_count,), route_count, jnp.int32)
        .at[position]
        .set(jnp.arange(route_count, dtype=jnp.int32), mode="drop")
    )
    occupied = source_route < route_count
    safe_route = jnp.where(occupied, source_route, 0)
    grad_held = jnp.where(occupied[:, None], out_grad[safe_route // top_count], 0)
    gate_held = jnp.where(occupied, gates.reshape(-1)[safe_route], 0.0).astype(jnp.bfloat16)
    grad_held = grad_held.reshape(slot_count, cap_rows, model_width)
    gate_held = gate_held.reshape(slot_count, cap_rows)
    got_rows, got_gate = (
        lax.all_to_all(grad_held, "expert", split_axis=0, concat_axis=0, tiled=True),
        lax.all_to_all(gate_held, "expert", split_axis=0, concat_axis=0, tiled=True),
    )
    flat_rows = got_rows.reshape(held_count, model_width)
    gate_f = got_gate.reshape(held_count, 1).astype(jnp.float32)
    held_hidden = saved_hidden.reshape(held_count, hidden_units)
    projected = lax.dot_general(
        flat_rows, down_weight[0], (((1,), (1,)), ((), ())), preferred_element_type=jnp.float32
    )
    hidden_grad = (gate_f * projected).astype(jnp.bfloat16)
    route_score = jnp.sum(projected * held_hidden.astype(jnp.float32), axis=1)
    returned = lax.all_to_all(
        route_score.reshape(slot_count, cap_rows), "expert", split_axis=0, concat_axis=0, tiled=True
    )
    score_flat = jnp.concatenate([returned.reshape(-1), jnp.zeros((1,), jnp.float32)])
    route_grad = jnp.where(kept_route, score_flat[position], 0.0).reshape(tok_dev, top_count)
    scaled = (gate_f * flat_rows.astype(jnp.float32)).astype(jnp.bfloat16)
    shard_rows = hidden_units // lax.axis_size("group")
    group_sum = lax.psum_scatter(
        lax.dot_general(
            held_hidden, scaled, (((0,), (0,)), ((), ())), preferred_element_type=jnp.float32
        ).astype(jnp.bfloat16),
        "group",
        scatter_dimension=0,
        tiled=True,
    )
    slot_ids, same_expert, ordinal = slot_layout(replica_plan)
    copies = jnp.sum(same_expert, axis=1)
    hot_first = (copies > 1) & (ordinal == 0)
    hot_rank = jnp.sum(hot_first[None, :] & (replica_plan[None, :] < replica_plan[:, None]), axis=1)
    my_slot = slot_ids == lax.axis_index("expert")
    my_rank = jnp.sum(jnp.where(my_slot, hot_rank, 0))
    my_hot = jnp.any(my_slot & (copies > 1))
    hot_ids = jnp.arange(HOT, dtype=jnp.int32)
    place_hot = (hot_ids == my_rank) & my_hot
    group_f = group_sum.astype(jnp.float32)
    table = jnp.where(place_hot[:, None, None], group_f[None], 0.0)
    summed = lax.psum(table.astype(jnp.bfloat16), "expert").astype(jnp.float32)
    picked = jnp.sum(jnp.where(place_hot[:, None, None], summed, 0.0), axis=0)
    copy_grad = jnp.where(my_hot, picked, group_f).astype(jnp.bfloat16)
    hidden_out = hidden_grad.reshape(1, 1, slot_count, cap_rows, hidden_units)
    return (route_grad, hidden_out, copy_grad.reshape(1, shard_rows, model_width))


def solution(mesh):
    placed = (
        P(("group", "expert"), None),
        P(("group", "expert"), None),
        P(("group", "expert"), None),
        P(("group", "expert"), None),
        P(),
        P("expert", None, None),
        P("group", "expert", None, None, None),
    )
    return jax.shard_map(
        local,
        mesh=mesh,
        in_specs=placed,
        out_specs=(
            P(("group", "expert"), None),
            P("group", "expert", None, None, None),
            P("expert", "group", None),
        ),
        check_vma=False,
    )
```

profile of v0, /device:TPU:2, one launch (start us, length us, event | category | flops | bytes accessed | tf_op | source)
XLA Modules:
  0.0 451.8 jit_solution(13898555410454085809)
XLA Ops:
  7.2 1.0 fusion.9
  10.5 0.8 add_select_fusion
  12.6 0.9 select_reduce_fusion.1
  14.6 9.1 %reduce-window.6 = s32[32,16,128]{2,1,0:T(8,128)S(1)} reduce-window(s32[32,16,128]{2,1,0:T(8,128)S(1)} %and_convert_fusion, s32[]{:T(128)} %constant.17.clone.1), window={size=1x1x128 pad=0_0x0_0x127_0}, to_apply=%region_2.3 | reduce-window | flops 8323072 | bytes 524292 | tf_op jit(solution)/shard_map/reduce-window
  24.4 0.8 fusion.7
  25.3 8.0 %scatter_custom_fusion = s32[640]{0:T(1024)S(1)} fusion(s32[2048]{0:T(1024)S(1)} %bitcast.45, s32[2048]{0:T(1024)S(1)} %iota.19, s32[]{:T(128)} %constant.20.clone.1), kind=kCustom, calls=%fused_computation.57 | custom fusion | bytes 2564 | tf_op jit(solution)/shard_map/scatter | solution.py:51
  33.3 4.3 gather_fusion.2
  38.4 11.5 %all-to-all-start.2 = ((bf16[32,1,20]{2,1,0:T(2,128)(2,1)}), bf16[32,1,20]{2,1,0:T(2,128)(2,1)S(1)}, u32[]{:S(2)}, u32[]{:S(2)}) async-start(bf16[32,1,20]{2,1,0:T(2,128)(2,1)} %all_to_all.20), calls=%async_computation.2 | async-start | bytes 32768 | tf_op jit(solution)/shard_map/all_to_all | solution.py:61
  50.0 5.1 %gather_fusion = bf16[640,3584]{1,0:T(8,128)(2,1)} fusion(bf16[256,3584]{1,0:T(8,128)(2,1)S(1)} %copy-done, s32[1024]{0:T(1024)S(1)} %pad_clamp_fusion.1), kind=kCustom, calls=%fused_computation | custom fusion | bytes 9177600 | tf_op jit(solution)/shard_map/gather | solution.py:55
  55.1 7.3 %gather.14 = bf16[32,20,3584]{2,1,0:T(8,128)(2,1)} reshape(bf16[640,3584]{1,0:T(8,128)(2,1)} %gather_fusion) | data formatting | bytes 9175040 | tf_op jit(solution)/shard_map/gather | solution.py:55
  62.4 5.4 %broadcast_select_fusion = bf16[32,20,3584]{2,1,0:T(8,128)(2,1)} fusion(bf16[32,20,3584]{2,1,0:T(8,128)(2,1)} %gather.14, pred[32,20]{1,0:T(8,128)(4,1)S(1)} %broadcast_in_dim.101), kind=kLoop, calls=%fused_computation.9 | loop fusion | flops 2293760 | bytes 9175680 | tf_op jit(solution)/shard_map/jit(_where)/select_n | solution.py:55
  67.9 9.9 %all-to-all-start = ((bf16[32,20,3584]{2,1,0:T(8,128)(2,1)}), bf16[32,20,3584]{2,1,0:T(8,128)(2,1)}, u32[]{:S(2)}, u32[]{:S(2)}) async-start(bf16[32,20,3584]{2,1,0:T(8,128)(2,1)} %broadcast_select_fusion), calls=%async_computation | async-start | bytes 11010048 | tf_op jit(solution)/shard_map/all_to_all | solution.py:60
  78.0 2.1 copy.58
  80.1 1.2 reshape.193
  81.3 118.0 %all-to-all-done = bf16[32,20,3584]{2,1,0:T(8,128)(2,1)} async-done(((bf16[32,20,3584]{2,1,0:T(8,128)(2,1)}), bf16[32,20,3584]{2,1,0:T(8,128)(2,1)}, u32[]{:S(2)}, u32[]{:S(2)}) %all-to-all-start) | async-done | bytes 4587552 | tf_op jit(solution)/shard_map/all_to_all | solution.py:60
  199.3 6.8 %multiply_convert_fusion = bf16[32,20,3584]{2,1,0:T(8,128)(2,1)} fusion(bf16[32,20,3584]{2,1,0:T(8,128)(2,1)} %all-to-all-done, f32[32,20]{1,0:T(8,128)S(1)} %bitcast.41), kind=kLoop, calls=%fused_computation.4 | loop fusion | flops 6881280 | bytes 9177600 | tf_op jit(solution)/shard_map/convert_element_type | solution.py:76
  206.0 7.4 %convert_element_type.91 = bf16[640,3584]{1,0:T(8,128)(2,1)} reshape(bf16[32,20,3584]{2,1,0:T(8,128)(2,1)} %multiply_convert_fusion) | data formatting | bytes 9175040 | tf_op jit(solution)/shard_map/convert_element_type | solution.py:76
  213.4 10.3 %fusion.2 = bf16[1024,3584]{0,1:T(8,128)(2,1)} fusion(bf16[640,3584]{1,0:T(8,128)(2,1)} %convert_element_type.91, bf16[640,1024]{1,0:T(8,128)(2,1)S(1)} %copy-done.3), kind=kOutput, calls=%fused_computation.8 | convolution fusion | flops 4701290496 | bytes 13238272 | tf_op jit(solution)/shard_map/dot_general | solution.py:79
  223.7 10.1 %copy.66 = bf16[1024,3584]{1,0:T(8,128)(2,1)} copy(bf16[1024,3584]{0,1:T(8,128)(2,1)} %fusion.2) | data formatting | bytes 14680064
  235.4 1.2 compare_and_fusion.2
  236.7 7.3 %reshape.192 = bf16[640,3584]{1,0:T(8,128)(2,1)} reshape(bf16[32,20,3584]{2,1,0:T(8,128)(2,1)} %all-to-all-done) | data formatting | bytes 9175040 | tf_op jit(solution)/shard_map/reshape | solution.py:63
  244.0 38.6 %reduce-scatter.4.cloned.1.call-done = bf16[128,3584]{1,0:T(8,128)(2,1)} async-done(((bf16[1024,3584]{1,0:T(8,128)(2,1)}), bf16[128,3584]{1,0:T(8,128)(2,1)}) %reduce-scatter.4.cloned.1.call-update) | async-done | bytes 917520 | tf_op jit(solution)/shard_map/reduce_scatter | solution.py:78
  282.6 2.7 select_convert_fusion
  285.4 10.5 %multiply_convert_fusion.1 = (bf16[640,1024]{1,0:T(8,128)(2,1)}, f32[640]{0:T(1024)S(1)}) fusion(f32[640]{0:T(1024)S(1)} %reshape.198, bf16[640,1024]{1,0:T(8,128)(2,1)S(1)} %copy-done.3, bf16[640,3584]{1,0:T(8,128)(2,1)} %reshape.192, bf16[1,1024,3584]{2,1,0:T(8,128)(2,1)} %param.12), kind=kOutput, calls=%fused_computation.12 | convolution fusion | flops 4700896768 | bytes 14554112 | tf_op jit(solution)/shard_map/dot_general | solution.py:66
  296.6 10.1 %all-to-all-start.1 = ((f32[32,1,20]{2,1,0:T(1,128)}), f32[32,1,20]{2,1,0:T(1,128)S(1)}, u32[]{:S(2)}, u32[]{:S(2)}) async-start(f32[32,1,20]{2,1,0:T(1,128)} %bitcast.6), calls=%async_computation.1 | async-start | bytes 32768 | tf_op jit(solution)/shard_map/all_to_all | solution.py:71
  306.8 2.2 reshape.196
  309.0 1.8 copy.64
  310.8 5.6 %all-to-all-done.1 = f32[32,1,20]{2,1,0:T(1,128)S(1)} async-done(((f32[32,1,20]{2,1,0:T(1,128)}), f32[32,1,20]{2,1,0:T(1,128)S(1)}, u32[]{:S(2)}, u32[]{:S(2)}) %all-to-all-start.1) | async-done | bytes 2592 | tf_op jit(solution)/shard_map/all_to_all | solution.py:71
  317.8 8.6 %gather_fusion.1 = f32[2048]{0:T(1024)S(1)} fusion(f32[641]{0:T(1024)S(1)} %pad_maximum_fusion, s32[2048]{0:T(1024)S(1)} %broadcast_clamp_fusion), kind=kCustom, calls=%fused_computation.1 | custom fusion | bytes 24576 | tf_op jit(solution)/shard_map/gather | solution.py:75
  327.2 114.1 %all-reduce.2.cloned.1.call-done = bf16[2,128,3584]{2,1,0:T(8,128)(2,1)} async-done(((bf16[2,128,3584]{2,1,0:T(8,128)(2,1)}), bf16[2,128,3584]{2,1,0:T(8,128)(2,1)}) %all-reduce.2.cloned.1.call-update) | async-done | bytes 1835024 | tf_op jit(solution)/shard_map/psum | solution.py:97
  441.3 2.0 select_reduce_fusion
  443.3 1.7 fusion.3
  (64 shorter events, 11.1 us)
Async XLA Ops:
  7.2 42.9 %copy-start = (bf16[256,3584]{1,0:T(8,128)(2,1)S(1)}, bf16[256,3584]{1,0:T(8,128)(2,1)}, u32[]{:S(2)}) copy-start(bf16[256,3584]{1,0:T(8,128)(2,1)} %param.7) | copy-start | bytes 5505028
  38.4 29.5 %all-to-all-start.2 = ((bf16[32,1,20]{2,1,0:T(2,128)(2,1)}), bf16[32,1,20]{2,1,0:T(2,128)(2,1)S(1)}, u32[]{:S(2)}, u32[]{:S(2)}) async-start(bf16[32,1,20]{2,1,0:T(2,128)(2,1)} %all_to_all.20), calls=%async_computation.2 | async-start | bytes 32768 | tf_op jit(solution)/shard_map/all_to_all | solution.py:61
  67.9 131.4 %all-to-all-start = ((bf16[32,20,3584]{2,1,0:T(8,128)(2,1)}), bf16[32,20,3584]{2,1,0:T(8,128)(2,1)}, u32[]{:S(2)}, u32[]{:S(2)}) async-start(bf16[32,20,3584]{2,1,0:T(8,128)(2,1)} %broadcast_select_fusion), calls=%async_computation | async-start | bytes 11010048 | tf_op jit(solution)/shard_map/all_to_all | solution.py:60
  77.8 204.9 %reduce-scatter.4.cloned.1.call-start = ((), (), s32[]{:S(2)}) async-start(), calls=%async_computation.5 | async-start | bytes 8257536 | tf_op jit(solution)/shard_map/reduce_scatter | solution.py:78
  206.0 7.4 %copy-start.3 = (bf16[640,1024]{1,0:T(8,128)(2,1)S(1)}, bf16[640,1024]{1,0:T(8,128)(2,1)}, u32[]{:S(2)}) copy-start(bf16[640,1024]{1,0:T(8,128)(2,1)} %reshape.193) | copy-start | bytes 3932164
  233.8 0.7 copy-start.4
  233.9 207.4 %all-reduce.2.cloned.1.call-start = ((), (), s32[]{:S(2)}) async-start(), calls=%async_computation.4 | async-start | bytes 3670016 | tf_op jit(solution)/shard_map/psum | solution.py:97
  296.6 19.8 %all-to-all-start.1 = ((f32[32,1,20]{2,1,0:T(1,128)}), f32[32,1,20]{2,1,0:T(1,128)S(1)}, u32[]{:S(2)}, u32[]{:S(2)}) async-start(f32[32,1,20]{2,1,0:T(1,128)} %bitcast.6), calls=%async_computation.1 | async-start | bytes 32768 | tf_op jit(solution)/shard_map/all_to_all | solution.py:71
  317.7 125.6 %copy-start.2 = (bf16[128,3584]{1,0:T(8,128)(2,1)S(1)}, bf16[128,3584]{1,0:T(8,128)(2,1)}, u32[]{:S(2)}) copy-start(bf16[128,3584]{1,0:T(8,128)(2,1)} %reduce-scatter.4.cloned.1.call-done) | copy-start | bytes 2752516
  317.8 127.3 %copy-start.1 = (bf16[256,3584]{1,0:T(8,128)(2,1)S(1)}, bf16[256,3584]{1,0:T(8,128)(2,1)}, u32[]{:S(2)}) copy-start(bf16[256,3584]{1,0:T(8,128)(2,1)} %param.7) | copy-start | bytes 5505028
Sparse Core Ops, SparseCore 0:
  234.0 48.5 reduce-scatter.3
  286.1 155.1 all-reduce.1
where the time goes:
time: 453 us; the launch traced here: 452 us
  waiting for transfers between devices  276 us (61%)
  local copies, waits for them, and re-layouts  71.8 us (16%)
  other arithmetic  36.7 us (8%)
  starting transfers between devices  31.7 us (7%)
  matrix products  20.8 us (5%)
  between operations  14.4 us (3%)
    all_to_all x1, waiting for transfers between devices, local(): lax.all_to_all(grad_held, 'expert', split_axis=0, concat_axis=0, tiled=True)  118 us
    psum x1, waiting for transfers between devices, local(): summed = lax.psum(table.astype(jnp.bfloat16), 'expert').astype(jnp.float32)  114 us
    reduce_scatter x1, waiting for transfers between devices, local(): lax.psum_scatter(lax.dot_general(held_hidden, scaled, (((0,), (0,)), ((),...  38.6 us
    unnamed x16, local copies, waits for them, and re-layouts  16.3 us
    gather x2, local copies, waits for them, and re-layouts, local(): out_grad[safe_route // top_count]  12.4 us
    all_to_all x1, starting transfers between devices, local(): lax.all_to_all(gate_held, 'expert', split_axis=0, concat_axis=0, tiled=True)  11.5 us
    dot_general x1, matrix products, local(): lax.dot_general(flat_rows, down_weight[0], (((1,), (1,)), ((), ())), pref...  10.5 us
    dot_general x1, matrix products, local(): lax.dot_general(held_hidden, scaled, (((0,), (0,)), ((), ())), preferred_...  10.3 us
  transfers between devices with their start and end apart: 5, of which 4 were waited for; matrix products, arithmetic and copies ran while one was open for 13% of the time, Pallas kernels for 0%

commit v1 on v0

--- a/solution.py
+++ b/solution.py
@@ -94,7 +94,9 @@
     place_hot = (hot_ids == my_rank) & my_hot
     group_f = group_sum.astype(jnp.float32)
     table = jnp.where(place_hot[:, None, None], group_f[None], 0.0)
-    summed = lax.psum(table.astype(jnp.bfloat16), "expert").astype(jnp.float32)
+    summed = jnp.sum(lax.all_gather(table.astype(jnp.bfloat16), "expert"), axis=0).astype(
+        jnp.float32
+    )
     picked = jnp.sum(jnp.where(place_hot[:, None, None], summed, 0.0), axis=0)
     copy_grad = jnp.where(my_hot, picked, group_f).astype(jnp.bfloat16)
     hidden_out = hidden_grad.reshape(1, 1, slot_count, cap_rows, hidden_units)

time: 453 us -> 703 us (1.55)
  waiting for transfers between devices: 276 us -> 507 us
  other arithmetic: 36.7 us -> 57.6 us
    all_gather x0 -> x1, waiting for transfers between devices: none -> 335 us  [local(): lax.all_gather(table.astype(jnp.bfloat16), 'expert')]
    psum x1 -> x0, waiting for transfers between devices: 114 us -> none  [local(): summed = lax.psum(table.astype(jnp.bfloat16), 'expert').astype(jnp.float32)]
    reduce_sum x0 -> x1, other arithmetic: none -> 20.6 us  [local(): jnp.sum(lax.all_gather(table.astype(jnp.bfloat16), 'expert'), axis=0)]
    reduce_scatter x1, waiting for transfers between devices: 38.6 us -> 45.9 us  [local(): lax.psum_scatter(lax.dot_general(held_hidden, scaled, (((0,), (0,)), ((),...]
  transfers between devices with their start and end apart: 5 -> 5, of which waited for: 4 -> 4; matrix products, arithmetic and copies ran while one was open for 13% -> 8% of each run, Pallas kernels for 0% -> 0%
where the time goes in v1:
time: 703 us; the launch traced here: 701 us
  waiting for transfers between devices  507 us (72%)
  local copies, waits for them, and re-layouts  69.4 us (10%)
  other arithmetic  57.6 us (8%)
  starting transfers between devices  32.1 us (5%)
  matrix products  20.9 us (3%)
  between operations  14.4 us (2%)
    all_gather x1, waiting for transfers between devices, local(): lax.all_gather(table.astype(jnp.bfloat16), 'expert')  335 us
    all_to_all x1, waiting for transfers between devices, local(): lax.all_to_all(grad_held, 'expert', split_axis=0, concat_axis=0, tiled=True)  120 us
    reduce_scatter x1, waiting for transfers between devices, local(): lax.psum_scatter(lax.dot_general(held_hidden, scaled, (((0,), (0,)), ((),...  45.9 us
    reduce_sum x1, other arithmetic, local(): jnp.sum(lax.all_gather(table.astype(jnp.bfloat16), 'expert'), axis=0)  20.6 us
    unnamed x16, local copies, waits for them, and re-layouts  14.9 us
  transfers between devices with their start and end apart: 5, of which 4 were waited for; matrix products, arithmetic and copies ran while one was open for 8% of the time, Pallas kernels for 0%

profile of v1, /device:TPU:2, one launch (start us, length us, event | category | flops | bytes accessed | tf_op | source)
XLA Modules:
  0.0 700.9 jit_solution(4196930401446239520)
XLA Ops:
  7.2 1.0 fusion.9
  10.5 0.8 add_select_fusion
  11.7 0.8 copy.60
  12.6 0.9 select_reduce_fusion.1
  14.6 9.1 %reduce-window.6 = s32[32,16,128]{2,1,0:T(8,128)S(1)} reduce-window(s32[32,16,128]{2,1,0:T(8,128)S(1)} %and_convert_fusion, s32[]{:T(128)} %constant.18.clone.1), window={size=1x1x128 pad=0_0x0_0x127_0}, to_apply=%region_2.3 | reduce-window | flops 8323072 | bytes 524292 | tf_op jit(solution)/shard_map/reduce-window
  24.4 0.8 fusion.7
  25.3 8.0 %scatter_custom_fusion = s32[640]{0:T(1024)S(1)} fusion(s32[2048]{0:T(1024)S(1)} %bitcast.45, s32[2048]{0:T(1024)S(1)} %iota.19, s32[]{:T(128)} %constant.23.clone.1), kind=kCustom, calls=%fused_computation.57 | custom fusion | bytes 2564 | tf_op jit(solution)/shard_map/scatter | solution.py:51
  33.3 4.3 gather_fusion.2
  38.4 11.5 %all-to-all-start.2 = ((bf16[32,1,20]{2,1,0:T(2,128)(2,1)}), bf16[32,1,20]{2,1,0:T(2,128)(2,1)S(1)}, u32[]{:S(2)}, u32[]{:S(2)}) async-start(bf16[32,1,20]{2,1,0:T(2,128)(2,1)} %all_to_all.20), calls=%async_computation.2 | async-start | bytes 32768 | tf_op jit(solution)/shard_map/all_to_all | solution.py:61
  50.0 5.1 gather_fusion
  55.2 7.2 %gather.14 = bf16[32,20,3584]{2,1,0:T(8,128)(2,1)} reshape(bf16[640,3584]{1,0:T(8,128)(2,1)} %gather_fusion) | data formatting | bytes 9175040 | tf_op jit(solution)/shard_map/gather | solution.py:55
  62.4 5.4 broadcast_select_fusion
  67.8 10.0 %all-to-all-start = ((bf16[32,20,3584]{2,1,0:T(8,128)(2,1)}), bf16[32,20,3584]{2,1,0:T(8,128)(2,1)}, u32[]{:S(2)}, u32[]{:S(2)}) async-start(bf16[32,20,3584]{2,1,0:T(8,128)(2,1)} %broadcast_select_fusion), calls=%async_computation | async-start | bytes 11010048 | tf_op jit(solution)/shard_map/all_to_all | solution.py:60
  79.1 120.2 %all-to-all-done = bf16[32,20,3584]{2,1,0:T(8,128)(2,1)} async-done(((bf16[32,20,3584]{2,1,0:T(8,128)(2,1)}), bf16[32,20,3584]{2,1,0:T(8,128)(2,1)}, u32[]{:S(2)}, u32[]{:S(2)}) %all-to-all-start) | async-done | bytes 4587552 | tf_op jit(solution)/shard_map/all_to_all | solution.py:60
  199.3 6.7 multiply_convert_fusion
  206.0 7.3 %convert_element_type.100 = bf16[640,3584]{1,0:T(8,128)(2,1)} reshape(bf16[32,20,3584]{2,1,0:T(8,128)(2,1)} %multiply_convert_fusion) | data formatting | bytes 9175040 | tf_op jit(solution)/shard_map/convert_element_type | solution.py:76
  213.3 10.3 %fusion.2 = bf16[1024,3584]{0,1:T(8,128)(2,1)} fusion(bf16[640,3584]{1,0:T(8,128)(2,1)} %convert_element_type.100, bf16[640,1024]{1,0:T(8,128)(2,1)S(1)} %reshape.199), kind=kOutput, calls=%fused_computation.8 | convolution fusion | flops 4701290496 | bytes 13238272 | tf_op jit(solution)/shard_map/dot_general | solution.py:79
  223.6 10.0 %copy.66 = bf16[1024,3584]{1,0:T(8,128)(2,1)} copy(bf16[1024,3584]{0,1:T(8,128)(2,1)} %fusion.2) | data formatting | bytes 14680064
  235.2 1.3 compare_and_fusion.2
  236.6 45.9 %reduce-scatter.4.cloned.1.call-done = bf16[128,3584]{1,0:T(8,128)(2,1)} async-done(((bf16[1024,3584]{1,0:T(8,128)(2,1)}), bf16[128,3584]{1,0:T(8,128)(2,1)}) %reduce-scatter.4.cloned.1.call-update) | async-done | bytes 917520 | tf_op jit(solution)/shard_map/reduce_scatter | solution.py:78
  282.4 2.8 select_convert_fusion
  285.4 7.3 %reshape.198 = bf16[640,3584]{1,0:T(8,128)(2,1)} reshape(bf16[32,20,3584]{2,1,0:T(8,128)(2,1)} %all-to-all-done) | data formatting | bytes 9175040 | tf_op jit(solution)/shard_map/reshape | solution.py:63
  292.7 10.5 %multiply_convert_fusion.1 = (bf16[640,1024]{1,0:T(8,128)(2,1)}, f32[640]{0:T(1024)S(1)}) fusion(f32[640]{0:T(1024)S(1)} %reshape.204, bf16[640,1024]{1,0:T(8,128)(2,1)S(1)} %reshape.199, bf16[640,3584]{1,0:T(8,128)(2,1)} %reshape.198, bf16[1,1024,3584]{2,1,0:T(8,128)(2,1)} %param.12), kind=kOutput, calls=%fused_computation.12 | convolution fusion | flops 4700896768 | bytes 14554112 | tf_op jit(solution)/shard_map/dot_general | solution.py:66
  303.9 10.3 %all-to-all-start.1 = ((f32[32,1,20]{2,1,0:T(1,128)}), f32[32,1,20]{2,1,0:T(1,128)S(1)}, u32[]{:S(2)}, u32[]{:S(2)}) async-start(f32[32,1,20]{2,1,0:T(1,128)} %bitcast.6), calls=%async_computation.1 | async-start | bytes 32768 | tf_op jit(solution)/shard_map/all_to_all | solution.py:71
  314.4 2.2 reshape.202
  316.6 1.8 copy.64
  318.4 5.4 all-to-all-done.1
  325.1 8.6 %gather_fusion.1 = f32[2048]{0:T(1024)S(1)} fusion(f32[641]{0:T(1024)S(1)} %pad_maximum_fusion, s32[2048]{0:T(1024)S(1)} %broadcast_clamp_fusion), kind=kCustom, calls=%fused_computation.1 | custom fusion | bytes 24576 | tf_op jit(solution)/shard_map/gather | solution.py:75
  334.5 335.1 %all-gather.2.cloned.1.call-done = bf16[32,2,128,3584]{3,2,1,0:T(8,128)(2,1)} async-done(((bf16[1,2,128,3584]{3,2,1,0:T(8,128)(2,1)}), bf16[32,2,128,3584]{3,2,1,0:T(8,128)(2,1)}) %all-gather.2.cloned.1.call-update) | async-done | bytes 58720272 | tf_op jit(solution)/shard_map/all_gather | solution.py:97
  669.6 20.6 %reduce_sum.108 = bf16[2,128,3584]{2,1,0:T(8,128)(2,1)} reduce(bf16[32,2,128,3584]{3,2,1,0:T(8,128)(2,1)} %all-gather.2.cloned.1.call-done, bf16[]{:T(256)} %constant.51.clone.1), dimensions={0}, to_apply=%region_13.14 | reduce | flops 28442624 | bytes 60555264 | tf_op jit(solution)/shard_map/reduce_sum | solution.py:97
  690.2 2.0 select_reduce_fusion
  692.2 1.9 fusion.3
  (65 shorter events, 11.4 us)
Async XLA Ops:
  7.2 42.9 %copy-start = (bf16[256,3584]{1,0:T(8,128)(2,1)S(1)}, bf16[256,3584]{1,0:T(8,128)(2,1)}, u32[]{:S(2)}) copy-start(bf16[256,3584]{1,0:T(8,128)(2,1)} %param.7) | copy-start | bytes 5505028
  38.4 29.4 %all-to-all-start.2 = ((bf16[32,1,20]{2,1,0:T(2,128)(2,1)}), bf16[32,1,20]{2,1,0:T(2,128)(2,1)S(1)}, u32[]{:S(2)}, u32[]{:S(2)}) async-start(bf16[32,1,20]{2,1,0:T(2,128)(2,1)} %all_to_all.20), calls=%async_computation.2 | async-start | bytes 32768 | tf_op jit(solution)/shard_map/all_to_all | solution.py:61
  67.8 10.3 %copy-start.3 = (bf16[1,1,32,20,1024]{4,2,3,1,0:T(8,128)(2,1)S(1)}, bf16[1,1,32,20,1024]{4,2,3,1,0:T(8,128)(2,1)}, u32[]{:S(2)}) copy-start(bf16[1,1,32,20,1024]{4,2,3,1,0:T(8,128)(2,1)} %param.13) | copy-start | bytes 3932164
  67.8 131.5 %all-to-all-start = ((bf16[32,20,3584]{2,1,0:T(8,128)(2,1)}), bf16[32,20,3584]{2,1,0:T(8,128)(2,1)}, u32[]{:S(2)}, u32[]{:S(2)}) async-start(bf16[32,20,3584]{2,1,0:T(8,128)(2,1)} %broadcast_select_fusion), calls=%async_computation | async-start | bytes 11010048 | tf_op jit(solution)/shard_map/all_to_all | solution.py:60
  77.8 204.6 %reduce-scatter.4.cloned.1.call-start = ((), (), s32[]{:S(2)}) async-start(), calls=%async_computation.5 | async-start | bytes 8257536 | tf_op jit(solution)/shard_map/reduce_scatter | solution.py:78
  233.6 0.8 copy-start.4
  233.7 436.0 %all-gather.2.cloned.1.call-start = ((), (), s32[]{:S(2)}) async-start(), calls=%async_computation.4 | async-start | bytes 60555264 | tf_op jit(solution)/shard_map/all_gather | solution.py:97
  303.9 19.8 %all-to-all-start.1 = ((f32[32,1,20]{2,1,0:T(1,128)}), f32[32,1,20]{2,1,0:T(1,128)S(1)}, u32[]{:S(2)}, u32[]{:S(2)}) async-start(f32[32,1,20]{2,1,0:T(1,128)} %bitcast.6), calls=%async_computation.1 | async-start | bytes 32768 | tf_op jit(solution)/shard_map/all_to_all | solution.py:71
  334.5 357.7 %copy-start.2 = (bf16[128,3584]{1,0:T(8,128)(2,1)S(1)}, bf16[128,3584]{1,0:T(8,128)(2,1)}, u32[]{:S(2)}) copy-start(bf16[128,3584]{1,0:T(8,128)(2,1)} %reduce-scatter.4.cloned.1.call-done) | copy-start | bytes 2752516
  669.6 24.5 %copy-start.1 = (bf16[256,3584]{1,0:T(8,128)(2,1)S(1)}, bf16[256,3584]{1,0:T(8,128)(2,1)}, u32[]{:S(2)}) copy-start(bf16[256,3584]{1,0:T(8,128)(2,1)} %param.7) | copy-start | bytes 5505028
Sparse Core Ops, SparseCore 0:
  233.8 48.6 reduce-scatter.3
  285.4 384.2 all-gather.1
